TPU v7x, 32 devices: a whole 2x2x4 slice. The times are simulated.
32 devices in a mesh: groups: 2 (over y), prefix: 4 (over z), heads: 2 (over x), sub: 2 (over core).
Axes of the slice: x: 2, y: 2, z: 4, core: 2. Of those that a mesh axis runs over, the one named last changes fastest.
Arguments:
- queries: bfloat16 [256, 8, 16, 128], P(('groups', 'prefix'), 'heads', 'sub'), parts along dimension 0, may hold values from -150 to 150
- prefix_keys: bfloat16 [16384, 8, 128], P(('groups', 'prefix'), 'heads'), parts along dimension 0, may hold values from -8 to 8
- prefix_values: bfloat16 [16384, 8, 128], P(('groups', 'prefix'), 'heads'), parts along dimension 0, may hold values from -9 to 9
- suffix_keys: bfloat16 [64, 1024, 8, 128], P(('groups', 'prefix'), None, 'heads'), parts along dimension 0, may hold values from -12 to 12
- suffix_values: bfloat16 [64, 1024, 8, 128], P(('groups', 'prefix'), None, 'heads'), parts along dimension 0, may hold values from -2 to 1
- accepted: int32 [64], P('groups'), parts along dimension 0, may hold values from 1 to 8, 128 in all
- cache_slot: int32 [64], P('groups'), parts along dimension 0, may hold values from 0 to 31, each once
- history: int32 [64], P('groups'), parts along dimension 0, may hold values from 128 to 1016
Outputs:
- attended: bfloat16 [256, 8, 16, 128], P(('groups', 'prefix'), 'heads', 'sub'), parts along dimension 0
There are 2 independent parts, one for each index of `groups`. A program takes and returns all parts, laid end to end along the dimension named above; each array names one. Nothing has to cross between parts.
Inputs may be any that keep to these rules, and one draw needn't show every extreme that they name: `accepted`: the counts sum to 128, and the largest count is 8. `cache_slot`: each slot is named by exactly one request; slot s lies on index s // 8 of prefix, at place s % 8.
All inputs are finite; a program needn't handle non-finite values.
Results may differ from a plain program's by a relative error of at most 0.005.
Values may be sent and summed in bfloat16 or wider, within the bound.
A program may use at most 128 MiB of HBM per device.

v0:
```python
import functools
import math

import jax
import jax.numpy as jnp
from jax import lax
from jax.experimental import pallas as pl
from jax.experimental.pallas import tpu as pltpu
from jax.sharding import PartitionSpec as P

MOST = 8
NEG = -1e30
LOG2E = 1.4426950408889634
VMEM = 67043328
SPARE = 12 * 1024 * 1024
MESH = pl.DeviceIdType.MESH


def nt_dot(a, b):
    return lax.dot_general(a, b, (((1,), (1,)), ((), ())), preferred_element_type=jnp.float32)


def greet(p, n):
    barrier = pltpu.get_barrier_semaphore()
    for step, there in ((-1, p > 0), (1, p < n - 1)):

        @pl.when(there)
        def _(step=step):
            pl.semaphore_signal(
                barrier, inc=1, device_id={"prefix": p + step}, device_id_type=MESH
            )

    pl.semaphore_wait(barrier, jnp.minimum(p, 1) + jnp.minimum(n - 1 - p, 1))


def grant(*held):
    kept = sum(math.prod(x.shape) * jnp.dtype(x.dtype).itemsize for x in held)
    return VMEM - kept - SPARE


def widen(raw, wide):
    wide[...] = raw.astype(jnp.float32)


def narrow(wide, h, heads):
    return wide[pl.ds(h, wide.shape[0] // heads, stride=heads), :].astype(jnp.bfloat16)


def prefix_pass(load_q, kd, vd, acc, den, top, at, scale, arrive):
    heads, plen, hd = kd.shape
    part = min(plen, 1024)
    pieces = plen // part
    stages = [(h, c) for h in range(heads) for c in range(pieces)]

    def score(stage):
        h, c = stage
        if c == 0:
            arrive(h)
        return nt_dot(load_q(h), kd[h, pl.ds(c * part, part), :])

    ready = score(stages[0])
    held = []
    for index, (h, c) in enumerate(stages):
        s = ready
        if index + 1 < len(stages):
            ready = score(stages[index + 1])
        m = jnp.max(s, axis=1, keepdims=True) * scale
        p = jnp.exp2(s * scale - m).astype(jnp.bfloat16)
        v = vd[h, pl.ds(c * part, part), :]
        pv = jnp.dot(
            p, jnp.concatenate([v, jnp.ones_like(v)], axis=1),
            preferred_element_type=jnp.float32,
        )
        held.append((m, pv))
        if c == pieces - 1:
            m, pv = held[0]
            for m_more, pv_more in held[1:]:
                joined = jnp.maximum(m, m_more)
                pv = pv * jnp.exp2(m - joined) + pv_more * jnp.exp2(m_more - joined)
                m = joined
            held = []
            _, count, gs, _ = acc.shape
            shape = (pv.shape[0] // gs, gs, hd)
            acc[h, at] = pv[:, :hd].reshape(shape)
            den[h, at] = pv[:, hd:].reshape(shape)
            top[h, at] = jnp.broadcast_to(m, (pv.shape[0], hd)).reshape(shape)


def gather_kernel(
    q_hbm, k_hbm, v_hbm, qall, acc, den, top,
    kraw, vraw, kwide, vwide, kd, vd, own_sem, raw_sem, send_sem, recv_sem, *, n, scale, pieces
):
    p = lax.axis_index("prefix")
    rows, heads, gs, hd = q_hbm.shape
    flat = k_hbm.shape[0]
    piece = flat // pieces
    unit = kwide.shape[0]

    def raw_copies(i):
        at = pl.ds(i * piece, piece)
        return (
            pltpu.make_async_copy(k_hbm.at[at], kraw.at[at], raw_sem.at[0, i]),
            pltpu.make_async_copy(v_hbm.at[at], vraw.at[at], raw_sem.at[1, i]),
        )

    def block_at(b):
        return pl.ds(b * rows, rows)

    def own_copy(h):
        return pltpu.make_async_copy(q_hbm.at[:, h], qall.at[h, block_at(p)], own_sem.at[h])

    def send(src, side, b, h):
        return pltpu.make_async_remote_copy(
            src_ref=src,
            dst_ref=qall.at[h, block_at(b)],
            send_sem=send_sem.at[side, b, h],
            recv_sem=recv_sem.at[b, h],
            device_id={"prefix": p + 1 if side == 0 else p - 1},
            device_id_type=MESH,
        )

    for i in range(pieces):
        for copy in raw_copies(i):
            copy.start()
    for h in range(heads):
        own_copy(h).start()
    greet(p, n)
    outward = ((0, p < n - 1), (1, p > 0))
    for h in range(heads):
        for side, there in outward:

            @pl.when(there)
            def _(side=side, h=h):
                send(q_hbm.at[:, h], side, p, h).start()

    for i in range(pieces):
        for copy in raw_copies(i):
            copy.wait()

        def split(u, carry, i=i):
            at = pl.ds(pl.multiple_of(i * piece + u * unit, unit), unit)
            per = unit // heads
            to = pl.ds(pl.multiple_of(i * (piece // heads) + u * per, per), per)
            widen(kraw[at], kwide)
            widen(vraw[at], vwide)
            for h in range(heads):
                kd[h, to] = narrow(kwide, h, heads)
                vd[h, to] = narrow(vwide, h, heads)
            return carry

        lax.fori_loop(0, piece // unit, split, 0)

    near = jnp.minimum(p, n - 1 - p)
    longer = jnp.where(p > n - 1 - p, -1, 1)

    def body(k, carry):
        paired = p + jnp.where(k % 2 == 1, -1, 1) * ((k + 1) // 2)
        single = p + longer * (k - near)
        b = jnp.where(k <= 2 * near, paired, single)

        def arrive(h):
            @pl.when(k == 0)
            def _():
                own_copy(h).wait()

            for side, there in outward:
                source = p - k if side == 0 else p + k
                landed = qall.at[h, block_at(source)]

                @pl.when((k > 0) & (source >= 0) & (source < n))
                def _(side=side, source=source, landed=landed, there=there):
                    send(landed, side, source, h).wait_recv()

                    @pl.when(there)
                    def _():
                        send(landed, side, source, h).start()

        def load_q(h):
            return qall[h, block_at(b)].reshape(rows * gs, hd)

        prefix_pass(load_q, kd, vd, acc, den, top, block_at(b), scale, arrive)
        return carry

    lax.fori_loop(0, n, body, 0)

    def drain(k, carry):
        for h in range(heads):
            for side, there in outward:
                source = p - k if side == 0 else p + k

                @pl.when(there & (source >= 0) & (source < n))
                def _(side=side, source=source, h=h):
                    send(qall.at[h, block_at(source)], side, source, h).wait_send()

        return carry

    lax.fori_loop(0, n, drain, 0)


def gathered(q, kf, vf, n):
    rows, heads, gs, hd = q.shape
    flat = kf.shape[0]
    plen = flat // heads
    pieces = 4
    unit = min(1024, flat // pieces)
    everything = (heads, n * rows, gs, hd)
    state = jax.ShapeDtypeStruct(everything, jnp.float32)
    vmem = pl.BlockSpec(memory_space=pltpu.VMEM)
    hbm = pl.BlockSpec(memory_space=pltpu.HBM)
    dma = pltpu.SemaphoreType.DMA
    shapes = [jax.ShapeDtypeStruct(everything, jnp.bfloat16), state, state, state]
    return pl.pallas_call(
        functools.partial(gather_kernel, n=n, scale=LOG2E / math.sqrt(hd), pieces=pieces),
        in_specs=[hbm, hbm, hbm],
        out_specs=[vmem] * 4,
        out_shape=shapes,
        scratch_shapes=[
            pltpu.VMEM((flat, hd), jnp.bfloat16),
            pltpu.VMEM((flat, hd), jnp.bfloat16),
            pltpu.VMEM((unit, hd), jnp.float32),
            pltpu.VMEM((unit, hd), jnp.float32),
            pltpu.VMEM((heads, plen, hd), jnp.bfloat16),
            pltpu.VMEM((heads, plen, hd), jnp.bfloat16),
            dma((heads,)),
            dma((2, pieces)),
            dma((2, n, heads)),
            dma((n, heads)),
        ],
        compiler_params=pltpu.CompilerParams(
            collective_id=0, has_side_effects=True, vmem_limit_bytes=grant(*shapes)
        ),
    )(q, kf, vf)


def suffix_kernel(
    accepted, cache_slot, history, qall, acc_in, den_in, top_in, sk_hbm, sv_hbm,
    acc, den, top, kbuf, vbuf, kwide, vwide, kd, vd, meta, tasks, sems, *, scale
):
    owner = lax.axis_index("prefix")
    heads, count, gs, hd = qall.shape
    slots, flat, _ = sk_hbm.shape
    depth, wide, _ = kbuf.shape
    chunk = wide // heads
    window = MOST * gs

    def find(r, start):
        amount = accepted[r]
        slot = cache_slot[r] - owner * slots

        @pl.when((slot >= 0) & (slot < slots))
        def _():
            meta[slot, 0] = start
            meta[slot, 1] = amount
            meta[slot, 2] = history[r]

        return start + amount

    lax.fori_loop(0, accepted.shape[0], find, jnp.int32(0))

    def copies(task, buf):
        slot = tasks[task, 0]
        src = pl.ds(pl.multiple_of(tasks[task, 1] * wide, wide), wide)
        return (
            pltpu.make_async_copy(sk_hbm.at[slot, src], kbuf.at[buf], sems.at[0, buf]),
            pltpu.make_async_copy(sv_hbm.at[slot, src], vbuf.at[buf], sems.at[1, buf]),
        )

    total = jnp.int32(0)
    for slot in range(slots):
        blocks = (meta[slot, 1] + meta[slot, 2] + chunk - 1) // chunk

        def put(i, at, slot=slot):
            tasks[at, 0] = slot
            tasks[at, 1] = i
            return at + 1

        total = lax.fori_loop(0, blocks, put, total)

    for ahead in range(depth - 1):

        @pl.when(ahead < total)
        def _(ahead=ahead):
            for copy in copies(ahead, ahead):
                copy.start()

    i_row = lax.broadcasted_iota(jnp.int32, (window, 1), 0) // gs
    pos = lax.broadcasted_iota(jnp.int32, (1, chunk), 1)

    def spread():
        for h in range(heads):
            kd[h] = narrow(kwide, h, heads)
            vd[h] = narrow(vwide, h, heads)

    @pl.when(total > 0)
    def _():
        for copy in copies(0, 0):
            copy.wait()
        widen(kbuf[0], kwide)
        widen(vbuf[0], vwide)
        spread()

    def body(t, carry):
        @pl.when(t + depth - 1 < total)
        def _():
            for copy in copies(t + depth - 1, lax.rem(t + depth - 1, depth)):
                copy.start()

        @pl.when(t + 1 < total)
        def _():
            for copy in copies(t + 1, lax.rem(t + 1, depth)):
                copy.wait()

        follow = lax.rem(t + 1, depth)
        widen(kbuf[follow], kwide)
        widen(vbuf[follow], vwide)

        slot = tasks[t, 0]
        base = tasks[t, 1] * chunk
        begin = meta[slot, 0]
        amount = meta[slot, 1]
        past = meta[slot, 2]
        start = jnp.minimum(begin, count - MOST)
        place = i_row + (start - begin)
        limit = jnp.where((place >= 0) & (place < amount), past + place + 1, 0) - base
        allowed = pos < limit
        rows_at = pl.ds(start, MOST)
        shape = (MOST, gs, hd)
        scores = [nt_dot(qall[h, rows_at].reshape(window, hd), kd[h]) for h in range(heads)]
        for h in range(heads):
            s = jnp.where(allowed, scores[h], NEG)
            old_top = top[h, rows_at].reshape(window, hd)
            m = jnp.maximum(old_top, jnp.max(s, axis=1, keepdims=True) * scale)
            p = jnp.exp2(s * scale - m[:, :1]).astype(jnp.bfloat16)
            v = vd[h]
            pv = jnp.dot(
                p, jnp.concatenate([v, jnp.ones_like(v)], axis=1),
                preferred_element_type=jnp.float32,
            )
            factor = jnp.exp2(old_top - m)
            top[h, rows_at] = m.reshape(shape)
            den[h, rows_at] = (
                den[h, rows_at].reshape(window, hd) * factor + pv[:, hd:]
            ).reshape(shape)
            acc[h, rows_at] = (
                acc[h, rows_at].reshape(window, hd) * factor + pv[:, :hd]
            ).reshape(shape)
        spread()
        return carry

    lax.fori_loop(0, total, body, 0)


def with_suffix(accepted, cache_slot, history, qall, acc, den, top, sk, sv):
    heads, count, gs, hd = qall.shape
    slots, flat, _ = sk.shape
    slen = flat // heads
    chunk = min(slen, 256)
    wide = chunk * heads
    depth = 4
    vmem = pl.BlockSpec(memory_space=pltpu.VMEM)
    hbm = pl.BlockSpec(memory_space=pltpu.HBM)
    smem = pl.BlockSpec(memory_space=pltpu.SMEM)
    return pl.pallas_call(
        functools.partial(suffix_kernel, scale=LOG2E / math.sqrt(hd)),
        in_specs=[smem] * 3 + [vmem] * 4 + [hbm] * 2,
        out_specs=[vmem] * 3,
        out_shape=[jax.ShapeDtypeStruct(acc.shape, jnp.float32)] * 3,
        input_output_aliases={4: 0, 5: 1, 6: 2},
        scratch_shapes=[
            pltpu.VMEM((depth, wide, hd), jnp.bfloat16),
            pltpu.VMEM((depth, wide, hd), jnp.bfloat16),
            pltpu.VMEM((wide, hd), jnp.float32),
            pltpu.VMEM((wide, hd), jnp.float32),
            pltpu.VMEM((heads, chunk, hd), jnp.bfloat16),
            pltpu.VMEM((heads, chunk, hd), jnp.bfloat16),
            pltpu.SMEM((slots, 3), jnp.int32),
            pltpu.SMEM((slots * (slen // chunk), 2), jnp.int32),
            pltpu.SemaphoreType.DMA((2, depth)),
        ],
        compiler_params=pltpu.CompilerParams(vmem_limit_bytes=grant(qall, acc, den, top)),
    )(accepted, cache_slot, history, qall, acc, den, top, sk, sv)


def reduce_kernel(
    acc, den, top, result, out_o, out_l, in_o, in_l, send_sem, recv_sem, *, n
):
    p = lax.axis_index("prefix")
    heads, count, gs, hd = acc.shape
    rows = count // n
    size = rows * gs
    groups = size // hd
    eye = lax.broadcasted_iota(jnp.int32, (1, hd, hd), 1) == lax.broadcasted_iota(
        jnp.int32, (1, hd, hd), 2
    )

    def sends(side, b, h):
        target = {"prefix": p + 1 if side == 0 else p - 1}
        return [
            pltpu.make_async_remote_copy(
                src_ref=out.at[b, h],
                dst_ref=into.at[side, b, h],
                send_sem=send_sem.at[kind, b, h],
                recv_sem=recv_sem.at[kind, side, b, h],
                device_id=target,
                device_id_type=MESH,
            )
            for kind, (out, into) in enumerate(((out_o, in_o), (out_l, in_l)))
        ]

    def own(b, h):
        at = pl.ds(b * rows, rows)
        return [ref[h, at].reshape(size, hd) for ref in (acc, den, top)]

    def joined(state, side, b, h):
        a, d, t = state
        o = in_o[side, b, h].astype(jnp.float32)
        lanes = jnp.broadcast_to(in_l[side, b, h][:, None, :], (groups, hd, hd))
        lse = jnp.sum(jnp.where(eye, lanes, 0.0), axis=2, keepdims=True).reshape(size, 1)
        m = jnp.maximum(t, lse)
        mine = jnp.exp2(t - m)
        theirs = jnp.exp2(lse - m)
        return a * mine + o * theirs, d * mine + theirs, m

    def pass_on(side, b, h, more):
        def emit(state):
            a, d, t = state
            out_o[b, h] = (a / d).astype(jnp.bfloat16)
            lse = (t + jnp.log2(d)).reshape(groups, hd, hd)
            out_l[b, h] = jnp.sum(jnp.where(eye, lse, 0.0), axis=1)

        @pl.when(more)
        def _():
            for copy in sends(side, b, h):
                copy.wait_recv()
            emit(joined(own(b, h), side, b, h))

        @pl.when(jnp.logical_not(more))
        def _():
            emit(own(b, h))

        for copy in sends(side, b, h):
            copy.start()

    greet(p, n)

    def step(j, carry):
        for h in range(heads):

            @pl.when(n - 1 - j > p)
            def _(h=h):
                pass_on(0, n - 1 - j, h, p > 0)

            @pl.when(j < p)
            def _(h=h):
                pass_on(1, j, h, p < n - 1)

        return carry

    lax.fori_loop(0, n - 1, step, 0)

    def finish(state, h):
        a, d, _ = state
        result[:, h] = (a / d).astype(result.dtype).reshape(rows, gs, hd)

    for h in range(heads):
        for side, there in ((0, p > 0), (1, p < n - 1)):

            @pl.when(there)
            def _(side=side, h=h):
                for copy in sends(side, p, h):
                    copy.wait_recv()

        @pl.when((p > 0) & (p < n - 1))
        def _(h=h):
            finish(joined(joined(own(p, h), 0, p, h), 1, p, h), h)

        @pl.when((p > 0) & (p == n - 1))
        def _(h=h):
            finish(joined(own(p, h), 0, p, h), h)

        @pl.when((p == 0) & (p < n - 1))
        def _(h=h):
            finish(joined(own(p, h), 1, p, h), h)

    def drain(j, carry):
        for h in range(heads):

            @pl.when(n - 1 - j > p)
            def _(h=h):
                for copy in sends(0, n - 1 - j, h):
                    copy.wait_send()

            @pl.when(j < p)
            def _(h=h):
                for copy in sends(1, j, h):
                    copy.wait_send()

        return carry

    lax.fori_loop(0, n - 1, drain, 0)


def reduced(acc, den, top, n):
    heads, count, gs, hd = acc.shape
    rows = count // n
    size = rows * gs
    dma = pltpu.SemaphoreType.DMA
    return pl.pallas_call(
        functools.partial(reduce_kernel, n=n),
        out_shape=jax.ShapeDtypeStruct((rows, heads, gs, hd), jnp.bfloat16),
        scratch_shapes=[
            pltpu.VMEM((n, heads, size, hd), jnp.bfloat16),
            pltpu.VMEM((n, heads, size // hd, hd), jnp.float32),
            pltpu.VMEM((2, n, heads, size, hd), jnp.bfloat16),
            pltpu.VMEM((2, n, heads, size // hd, hd), jnp.float32),
            dma((2, n, heads)),
            dma((2, 2, n, heads)),
        ],
        compiler_params=pltpu.CompilerParams(
            collective_id=1, has_side_effects=True, vmem_limit_bytes=32 * 1024 * 1024
        ),
    )(acc, den, top)


def local(
    queries, prefix_keys, prefix_values, suffix_keys, suffix_values, accepted, cache_slot, history
):
    n = lax.axis_size("prefix")
    plen, heads, hd = prefix_keys.shape
    slots, slen, _, _ = suffix_keys.shape
    kf = prefix_keys.reshape(plen * heads, hd)
    vf = prefix_values.reshape(plen * heads, hd)
    sk = suffix_keys.reshape(slots, slen * heads, hd)
    sv = suffix_values.reshape(slots, slen * heads, hd)
    qall, acc, den, top = gathered(queries, kf, vf, n)
    acc, den, top = with_suffix(accepted, cache_slot, history, qall, acc, den, top, sk, sv)
    return reduced(acc, den, top, n)


def solution(mesh):
    in_specs = (
        P(("groups", "prefix"), "heads", "sub", None),
        P(("groups", "prefix"), "heads", None),
        P(("groups", "prefix"), "heads", None),
        P(("groups", "prefix"), None, "heads", None),
        P(("groups", "prefix"), None, "heads", None),
        P("groups"),
        P("groups"),
        P("groups"),
    )
    out_specs = P(("groups", "prefix"), "heads", "sub", None)
    return jax.shard_map(local, mesh=mesh, in_specs=in_specs, out_specs=out_specs, check_vma=False)
```

profile of v0, /device:TPU:22, one launch (start us, length us, event | category | flops | bytes accessed | tf_op | source)
XLA Modules:
  0.0 81.6 jit_solution(1912296443573098191)
XLA Ops:
  0.0 0.0 copy-start
  0.0 0.9 %copy-done = bf16[32,4,8,128]{3,2,1,0:T(8,128)(2,1)S(1)} copy-done((bf16[32,4,8,128]{3,2,1,0:T(8,128)(2,1)S(1)}, bf16[32,4,8,128]{3,2,1,0:T(8,128)(2,1)}, u32[]{:S(2)}) %copy-start) | copy-done | bytes 262168
  1.0 0.0 copy-start.1
  1.0 0.0 copy-start.2
  1.0 0.0 copy-start.3
  1.0 19.5 %shard_map.82 = (bf16[4,128,8,128]{3,2,1,0:T(8,128)(2,1)S(1)}, f32[4,128,8,128]{3,2,1,0:T(8,128)S(1)}, f32[4,128,8,128]{3,2,1,0:T(8,128)S(1)}, f32[4,128,8,128]{3,2,1,0:T(8,128)S(1)}) custom-call(bf16[32,4,8,128]{3,2,1,0:T(8,128)(2,1)S(1)} %copy-done, bf16[8192,128]{1,0:T(8,128)(2,1)} %bitcast.6, bf16[8192,128]{1,0:T(8,128)(2,1)} %bitcast.7), custom_call_target="tpu_custom_call" | custom-call | tf_op jit(solution)/shard_map/pallas_call | solution.py:212
  20.5 0.0 copy-done.1
  20.5 0.0 copy-done.2
  20.5 0.0 copy-done.3
  20.5 16.9 %shard_map.83 = (f32[4,128,8,128]{3,2,1,0:T(8,128)S(1)}, f32[4,128,8,128]{3,2,1,0:T(8,128)S(1)}, f32[4,128,8,128]{3,2,1,0:T(8,128)S(1)}) custom-call(s32[32]{0:T(128)S(1)} %copy-done.1, s32[32]{0:T(128)S(1)} %copy-done.2, s32[32]{0:T(128)S(1)} %copy-done.3, ...), custom_call_target="tpu_custom_call", output_to_operand_aliasing={{0}: (4, {}), {1}: (5, {}), {2}: (6, {})} | custom-call | tf_op jit(solution)/shard_map/pallas_call | solution.py:363
  37.4 43.5 %shard_map.84 = bf16[32,4,8,128]{3,2,1,0:T(8,128)(2,1)S(1)} custom-call(f32[4,128,8,128]{3,2,1,0:T(8,128)S(1)} %get-tuple-element.16.acc, f32[4,128,8,128]{3,2,1,0:T(8,128)S(1)} %get-tuple-element.17.den, f32[4,128,8,128]{3,2,1,0:T(8,128)S(1)} %get-tuple-element.18.top), custom_call_target="tpu_custom_call" | custom-call | tf_op jit(solution)/shard_map/pallas_call | solution.py:508
  80.9 0.7 copy.16
Async XLA Ops:
  0.0 0.9 %copy-start = (bf16[32,4,8,128]{3,2,1,0:T(8,128)(2,1)S(1)}, bf16[32,4,8,128]{3,2,1,0:T(8,128)(2,1)}, u32[]{:S(2)}) copy-start(bf16[32,4,8,128]{3,2,1,0:T(8,128)(2,1)} %q_hbm.1) | copy-start | bytes 786436
  1.0 19.5 %copy-start.1 = (s32[32]{0:T(128)S(1)}, s32[32]{0:T(128)}, u32[]{:S(2)}) copy-start(s32[32]{0:T(128)} %accepted.1) | copy-start | bytes 388
  1.0 19.6 %copy-start.2 = (s32[32]{0:T(128)S(1)}, s32[32]{0:T(128)}, u32[]{:S(2)}) copy-start(s32[32]{0:T(128)} %cache_slot.1) | copy-start | bytes 388
  1.0 19.6 %copy-start.3 = (s32[32]{0:T(128)S(1)}, s32[32]{0:T(128)}, u32[]{:S(2)}) copy-start(s32[32]{0:T(128)} %history.1) | copy-start | bytes 388
where the time goes:
time: 82.2 us; the launch traced here: 81.6 us
  Pallas kernels  79.9 us (97%)
  local copies, waits for them, and re-layouts  1.67 us (2%)
    pallas_call x1, Pallas kernels, reduced(): pl.pallas_call(functools.partial(reduce_kernel, n=n), out_shape=jax.Shape...  43.5 us
    pallas_call x1, Pallas kernels, gathered(): pl.pallas_call(functools.partial(gather_kernel, n=n, scale=LOG2E / math.s...  19.5 us
    pallas_call x1, Pallas kernels, with_suffix(): pl.pallas_call(functools.partial(suffix_kernel, scale=LOG2E / math.sqrt(h...  16.9 us
    unnamed x9, local copies, waits for them, and re-layouts  1.67 us

commit v1 on v0

--- a/solution.py
+++ b/solution.py
@@ -10,8 +10,10 @@
 
 MOST = 8
 NEG = -1e30
+FLOOR = -1e29
 LOG2E = 1.4426950408889634
 VMEM = 67043328
+STAGGER = 2
 SPARE = 12 * 1024 * 1024
 MESH = pl.DeviceIdType.MESH
 
@@ -234,7 +236,8 @@
 
 def suffix_kernel(
     accepted, cache_slot, history, qall, acc_in, den_in, top_in, sk_hbm, sv_hbm,
-    acc, den, top, kbuf, vbuf, kwide, vwide, kd, vd, meta, tasks, sems, *, scale
+    acc, den, top, kbuf, vbuf, kwide, vwide, kwide_b, vwide_b, kd, vd, kd_b, vd_b, meta, tasks, sems,
+    *, scale
 ):
     owner = lax.axis_index("prefix")
     heads, count, gs, hd = qall.shape
@@ -276,78 +279,92 @@
 
         total = lax.fori_loop(0, blocks, put, total)
 
-    for ahead in range(depth - 1):
-
-        @pl.when(ahead < total)
-        def _(ahead=ahead):
-            for copy in copies(ahead, ahead):
+    def begin_copy(task):
+        @pl.when(task < total)
+        def _():
+            for copy in copies(task, lax.rem(task, depth)):
                 copy.start()
+
+    def finish_copy(task):
+        @pl.when(task < total)
+        def _():
+            for copy in copies(task, lax.rem(task, depth)):
+                copy.wait()
+
+    for task in range(depth - 1):
+        begin_copy(jnp.int32(task))
 
     i_row = lax.broadcasted_iota(jnp.int32, (window, 1), 0) // gs
     pos = lax.broadcasted_iota(jnp.int32, (1, chunk), 1)
-
-    def spread():
+    shape = (MOST, gs, hd)
+
+    def load(task, kwide, vwide):
+        buf = lax.rem(task, depth)
+        widen(kbuf[buf], kwide)
+        widen(vbuf[buf], vwide)
+
+    def spread(kwide, vwide, kd, vd):
         for h in range(heads):
             kd[h] = narrow(kwide, h, heads)
             vd[h] = narrow(vwide, h, heads)
 
-    @pl.when(total > 0)
-    def _():
-        for copy in copies(0, 0):
-            copy.wait()
-        widen(kbuf[0], kwide)
-        widen(vbuf[0], vwide)
-        spread()
-
-    def body(t, carry):
-        @pl.when(t + depth - 1 < total)
-        def _():
-            for copy in copies(t + depth - 1, lax.rem(t + depth - 1, depth)):
-                copy.start()
-
-        @pl.when(t + 1 < total)
-        def _():
-            for copy in copies(t + 1, lax.rem(t + 1, depth)):
-                copy.wait()
-
-        follow = lax.rem(t + 1, depth)
-        widen(kbuf[follow], kwide)
-        widen(vbuf[follow], vwide)
-
-        slot = tasks[t, 0]
-        base = tasks[t, 1] * chunk
+    def attend(task, kd, vd):
+        real = task < total
+        known = jnp.minimum(task, total - 1)
+        slot = tasks[known, 0]
+        base = tasks[known, 1] * chunk
         begin = meta[slot, 0]
-        amount = meta[slot, 1]
+        amount = jnp.where(real, meta[slot, 1], 0)
         past = meta[slot, 2]
         start = jnp.minimum(begin, count - MOST)
         place = i_row + (start - begin)
         limit = jnp.where((place >= 0) & (place < amount), past + place + 1, 0) - base
         allowed = pos < limit
         rows_at = pl.ds(start, MOST)
-        shape = (MOST, gs, hd)
         scores = [nt_dot(qall[h, rows_at].reshape(window, hd), kd[h]) for h in range(heads)]
+        parts = []
         for h in range(heads):
             s = jnp.where(allowed, scores[h], NEG)
-            old_top = top[h, rows_at].reshape(window, hd)
-            m = jnp.maximum(old_top, jnp.max(s, axis=1, keepdims=True) * scale)
-            p = jnp.exp2(s * scale - m[:, :1]).astype(jnp.bfloat16)
+            m = jnp.maximum(jnp.max(s, axis=1, keepdims=True), FLOOR) * scale
+            p = jnp.exp2(s * scale - m).astype(jnp.bfloat16)
             v = vd[h]
             pv = jnp.dot(
                 p, jnp.concatenate([v, jnp.ones_like(v)], axis=1),
                 preferred_element_type=jnp.float32,
             )
-            factor = jnp.exp2(old_top - m)
-            top[h, rows_at] = m.reshape(shape)
+            parts.append((m, pv))
+        for h, (m, pv) in enumerate(parts):
+            old = top[h, rows_at].reshape(window, hd)
+            new = jnp.maximum(old, m)
+            keep = jnp.exp2(old - new)
+            gain = jnp.exp2(m - new)
+            top[h, rows_at] = new.reshape(shape)
             den[h, rows_at] = (
-                den[h, rows_at].reshape(window, hd) * factor + pv[:, hd:]
+                den[h, rows_at].reshape(window, hd) * keep + pv[:, hd:] * gain
             ).reshape(shape)
             acc[h, rows_at] = (
-                acc[h, rows_at].reshape(window, hd) * factor + pv[:, :hd]
+                acc[h, rows_at].reshape(window, hd) * keep + pv[:, :hd] * gain
             ).reshape(shape)
-        spread()
+
+    finish_copy(jnp.int32(0))
+    load(jnp.int32(0), kwide, vwide)
+    spread(kwide, vwide, kd, vd)
+
+    def body(i, carry):
+        t = 2 * i
+        begin_copy(t + 3)
+        begin_copy(t + 4)
+        finish_copy(t + 1)
+        finish_copy(t + 2)
+        load(t + 1, kwide_b, vwide_b)
+        attend(t, kd, vd)
+        spread(kwide_b, vwide_b, kd_b, vd_b)
+        load(t + 2, kwide, vwide)
+        attend(t + 1, kd_b, vd_b)
+        spread(kwide, vwide, kd, vd)
         return carry
 
-    lax.fori_loop(0, total, body, 0)
+    lax.fori_loop(0, (total + 1) // 2, body, 0)
 
 
 def with_suffix(accepted, cache_slot, history, qall, acc, den, top, sk, sv):
@@ -369,10 +386,10 @@
         scratch_shapes=[
             pltpu.VMEM((depth, wide, hd), jnp.bfloat16),
             pltpu.VMEM((depth, wide, hd), jnp.bfloat16),
-            pltpu.VMEM((wide, hd), jnp.float32),
-            pltpu.VMEM((wide, hd), jnp.float32),
-            pltpu.VMEM((heads, chunk, hd), jnp.bfloat16),
-            pltpu.VMEM((heads, chunk, hd), jnp.bfloat16),
+        ]
+        + [pltpu.VMEM((wide, hd), jnp.float32)] * 4
+        + [pltpu.VMEM((heads, chunk, hd), jnp.bfloat16)] * 4
+        + [
             pltpu.SMEM((slots, 3), jnp.int32),
             pltpu.SMEM((slots * (slen // chunk), 2), jnp.int32),
             pltpu.SemaphoreType.DMA((2, depth)),
@@ -443,20 +460,25 @@
 
     greet(p, n)
 
-    def step(j, carry):
-        for h in range(heads):
-
-            @pl.when(n - 1 - j > p)
-            def _(h=h):
-                pass_on(0, n - 1 - j, h, p > 0)
-
-            @pl.when(j < p)
-            def _(h=h):
-                pass_on(1, j, h, p < n - 1)
+    chunks = (n - 1) * heads
+
+    def step(t, carry):
+        right = t - STAGGER * p
+        left = t - STAGGER * (n - 1 - p)
+        ahead = n - 1 - right // heads
+        behind = left // heads
+
+        @pl.when((right >= 0) & (right < chunks) & (ahead > p))
+        def _():
+            pass_on(0, ahead, right % heads, p > 0)
+
+        @pl.when((left >= 0) & (left < chunks) & (behind < p))
+        def _():
+            pass_on(1, behind, left % heads, p < n - 1)
 
         return carry
 
-    lax.fori_loop(0, n - 1, step, 0)
+    lax.fori_loop(0, chunks + STAGGER * (n - 1), step, 0)
 
     def finish(state, h):
         a, d, _ = state

time: 82.2 us -> 59.8 us (0.73)
  the two profiles are of different devices: /device:TPU:22 before, /device:TPU:0 now
where the time goes in v1:
time: 59.8 us; the launch traced here: 60.5 us
  Pallas kernels  58.8 us (98%)
  local copies, waits for them, and re-layouts  1.67 us (3%)
    pallas_call x1, Pallas kernels, gathered(): pl.pallas_call(functools.partial(gather_kernel, n=n, scale=LOG2E / math.s...  24 us
    pallas_call x1, Pallas kernels, reduced(): pl.pallas_call(functools.partial(reduce_kernel, n=n), out_shape=jax.Shape...  18 us
    pallas_call x1, Pallas kernels, with_suffix(): pl.pallas_call(functools.partial(suffix_kernel, scale=LOG2E / math.sqrt(h...  16.8 us
    unnamed x9, local copies, waits for them, and re-layouts  1.67 us

profile of v1, /device:TPU:0, one launch (start us, length us, event | category | flops | bytes accessed | tf_op | source)
XLA Modules:
  0.0 60.5 jit_solution(3085133378894639057)
XLA Ops:
  0.0 0.0 copy-start
  0.0 0.9 %copy-done = bf16[32,4,8,128]{3,2,1,0:T(8,128)(2,1)S(1)} copy-done((bf16[32,4,8,128]{3,2,1,0:T(8,128)(2,1)S(1)}, bf16[32,4,8,128]{3,2,1,0:T(8,128)(2,1)}, u32[]{:S(2)}) %copy-start) | copy-done | bytes 262168
  1.0 0.0 copy-start.1
  1.0 0.0 copy-start.2
  1.0 0.0 copy-start.3
  1.0 24.0 %shard_map.82 = (bf16[4,128,8,128]{3,2,1,0:T(8,128)(2,1)S(1)}, f32[4,128,8,128]{3,2,1,0:T(8,128)S(1)}, f32[4,128,8,128]{3,2,1,0:T(8,128)S(1)}, f32[4,128,8,128]{3,2,1,0:T(8,128)S(1)}) custom-call(bf16[32,4,8,128]{3,2,1,0:T(8,128)(2,1)S(1)} %copy-done, bf16[8192,128]{1,0:T(8,128)(2,1)} %bitcast.6, bf16[8192,128]{1,0:T(8,128)(2,1)} %bitcast.7), custom_call_target="tpu_custom_call" | custom-call | tf_op jit(solution)/shard_map/pallas_call | solution.py:214
  24.9 0.0 copy-done.1
  24.9 0.0 copy-done.2
  25.0 0.0 copy-done.3
  25.0 16.8 %shard_map.83 = (f32[4,128,8,128]{3,2,1,0:T(8,128)S(1)}, f32[4,128,8,128]{3,2,1,0:T(8,128)S(1)}, f32[4,128,8,128]{3,2,1,0:T(8,128)S(1)}) custom-call(s32[32]{0:T(128)S(1)} %copy-done.1, s32[32]{0:T(128)S(1)} %copy-done.2, s32[32]{0:T(128)S(1)} %copy-done.3, ...), custom_call_target="tpu_custom_call", output_to_operand_aliasing={{0}: (4, {}), {1}: (5, {}), {2}: (6, {})} | custom-call | tf_op jit(solution)/shard_map/pallas_call | solution.py:380
  41.7 18.0 %shard_map.84 = bf16[32,4,8,128]{3,2,1,0:T(8,128)(2,1)S(1)} custom-call(f32[4,128,8,128]{3,2,1,0:T(8,128)S(1)} %get-tuple-element.16.acc, f32[4,128,8,128]{3,2,1,0:T(8,128)S(1)} %get-tuple-element.17.den, f32[4,128,8,128]{3,2,1,0:T(8,128)S(1)} %get-tuple-element.18.top), custom_call_target="tpu_custom_call" | custom-call | tf_op jit(solution)/shard_map/pallas_call | solution.py:530
  59.8 0.7 %copy.16 = bf16[32,4,8,128]{3,2,1,0:T(8,128)(2,1)} copy(bf16[32,4,8,128]{3,2,1,0:T(8,128)(2,1)S(1)} %shard_map.84) | data formatting | bytes 524288
Async XLA Ops:
  0.0 0.9 %copy-start = (bf16[32,4,8,128]{3,2,1,0:T(8,128)(2,1)S(1)}, bf16[32,4,8,128]{3,2,1,0:T(8,128)(2,1)}, u32[]{:S(2)}) copy-start(bf16[32,4,8,128]{3,2,1,0:T(8,128)(2,1)} %q_hbm.1) | copy-start | bytes 786436
  1.0 24.0 %copy-start.1 = (s32[32]{0:T(128)S(1)}, s32[32]{0:T(128)}, u32[]{:S(2)}) copy-start(s32[32]{0:T(128)} %accepted.1) | copy-start | bytes 388
  1.0 24.0 %copy-start.2 = (s32[32]{0:T(128)S(1)}, s32[32]{0:T(128)}, u32[]{:S(2)}) copy-start(s32[32]{0:T(128)} %cache_slot.1) | copy-start | bytes 388
  1.0 24.0 %copy-start.3 = (s32[32]{0:T(128)S(1)}, s32[32]{0:T(128)}, u32[]{:S(2)}) copy-start(s32[32]{0:T(128)} %history.1) | copy-start | bytes 388

commit v2 on v1

--- a/solution.py
+++ b/solution.py
@@ -14,6 +14,8 @@
 LOG2E = 1.4426950408889634
 VMEM = 67043328
 STAGGER = 2
+BATCH = 4
+LOOK = 2
 SPARE = 12 * 1024 * 1024
 MESH = pl.DeviceIdType.MESH
 
@@ -236,8 +238,7 @@
 
 def suffix_kernel(
     accepted, cache_slot, history, qall, acc_in, den_in, top_in, sk_hbm, sv_hbm,
-    acc, den, top, kbuf, vbuf, kwide, vwide, kwide_b, vwide_b, kd, vd, kd_b, vd_b, meta, tasks, sems,
-    *, scale
+    acc, den, top, kbuf, vbuf, kwide, vwide, kd, vd, meta, tasks, sems, *, scale
 ):
     owner = lax.axis_index("prefix")
     heads, count, gs, hd = qall.shape
@@ -246,20 +247,6 @@
     chunk = wide // heads
     window = MOST * gs
 
-    def find(r, start):
-        amount = accepted[r]
-        slot = cache_slot[r] - owner * slots
-
-        @pl.when((slot >= 0) & (slot < slots))
-        def _():
-            meta[slot, 0] = start
-            meta[slot, 1] = amount
-            meta[slot, 2] = history[r]
-
-        return start + amount
-
-    lax.fori_loop(0, accepted.shape[0], find, jnp.int32(0))
-
     def copies(task, buf):
         slot = tasks[task, 0]
         src = pl.ds(pl.multiple_of(tasks[task, 1] * wide, wide), wide)
@@ -268,7 +255,27 @@
             pltpu.make_async_copy(sv_hbm.at[slot, src], vbuf.at[buf], sems.at[1, buf]),
         )
 
-    total = jnp.int32(0)
+    for slot in range(slots):
+        tasks[slot, 0] = slot
+        tasks[slot, 1] = 0
+        for copy in copies(slot, slot):
+            copy.start()
+
+    def find(r, start):
+        amount = accepted[r]
+        slot = cache_slot[r] - owner * slots
+
+        @pl.when((slot >= 0) & (slot < slots))
+        def _():
+            meta[slot, 0] = start
+            meta[slot, 1] = amount
+            meta[slot, 2] = history[r]
+
+        return start + amount
+
+    lax.fori_loop(0, accepted.shape[0], find, jnp.int32(0))
+
+    total = jnp.int32(slots)
     for slot in range(slots):
         blocks = (meta[slot, 1] + meta[slot, 2] + chunk - 1) // chunk
 
@@ -277,7 +284,7 @@
             tasks[at, 1] = i
             return at + 1
 
-        total = lax.fori_loop(0, blocks, put, total)
+        total = lax.fori_loop(1, blocks, put, total)
 
     def begin_copy(task):
         @pl.when(task < total)
@@ -291,49 +298,51 @@
             for copy in copies(task, lax.rem(task, depth)):
                 copy.wait()
 
-    for task in range(depth - 1):
+    for task in range(slots, depth):
         begin_copy(jnp.int32(task))
 
     i_row = lax.broadcasted_iota(jnp.int32, (window, 1), 0) // gs
     pos = lax.broadcasted_iota(jnp.int32, (1, chunk), 1)
     shape = (MOST, gs, hd)
 
-    def load(task, kwide, vwide):
-        buf = lax.rem(task, depth)
-        widen(kbuf[buf], kwide)
-        widen(vbuf[buf], vwide)
-
-    def spread(kwide, vwide, kd, vd):
+    def spread(task, k):
+        buf = lax.rem(jnp.minimum(task, total - 1), depth)
+        widen(kbuf[buf], kwide.at[k])
+        widen(vbuf[buf], vwide.at[k])
         for h in range(heads):
-            kd[h] = narrow(kwide, h, heads)
-            vd[h] = narrow(vwide, h, heads)
-
-    def attend(task, kd, vd):
-        real = task < total
+            kd[k, h] = narrow(kwide.at[k], h, heads)
+            vd[k, h] = narrow(vwide.at[k], h, heads)
+
+    def place_of(task):
         known = jnp.minimum(task, total - 1)
         slot = tasks[known, 0]
         base = tasks[known, 1] * chunk
         begin = meta[slot, 0]
-        amount = jnp.where(real, meta[slot, 1], 0)
+        amount = jnp.where(task < total, meta[slot, 1], 0)
         past = meta[slot, 2]
         start = jnp.minimum(begin, count - MOST)
         place = i_row + (start - begin)
         limit = jnp.where((place >= 0) & (place < amount), past + place + 1, 0) - base
-        allowed = pos < limit
-        rows_at = pl.ds(start, MOST)
-        scores = [nt_dot(qall[h, rows_at].reshape(window, hd), kd[h]) for h in range(heads)]
-        parts = []
-        for h in range(heads):
-            s = jnp.where(allowed, scores[h], NEG)
-            m = jnp.maximum(jnp.max(s, axis=1, keepdims=True), FLOOR) * scale
-            p = jnp.exp2(s * scale - m).astype(jnp.bfloat16)
-            v = vd[h]
-            pv = jnp.dot(
-                p, jnp.concatenate([v, jnp.ones_like(v)], axis=1),
-                preferred_element_type=jnp.float32,
-            )
-            parts.append((m, pv))
-        for h, (m, pv) in enumerate(parts):
+        return pl.ds(start, MOST), limit
+
+    def body(i, carry):
+        first = i * BATCH
+        for k in range(BATCH):
+            finish_copy(first + k)
+        for k in range(BATCH):
+            spread(first + k, k)
+        for k in range(BATCH):
+            begin_copy(first + depth + k)
+        spots = [place_of(first + k) for k in range(BATCH)]
+        stages = [(k, h) for k in range(BATCH) for h in range(heads)]
+
+        def score(stage):
+            k, h = stage
+            return nt_dot(qall[h, spots[k][0]].reshape(window, hd), kd[k, h])
+
+        def fold(stage, m, pv):
+            k, h = stage
+            rows_at = spots[k][0]
             old = top[h, rows_at].reshape(window, hd)
             new = jnp.maximum(old, m)
             keep = jnp.exp2(old - new)
@@ -346,25 +355,22 @@
                 acc[h, rows_at].reshape(window, hd) * keep + pv[:, :hd] * gain
             ).reshape(shape)
 
-    finish_copy(jnp.int32(0))
-    load(jnp.int32(0), kwide, vwide)
-    spread(kwide, vwide, kd, vd)
-
-    def body(i, carry):
-        t = 2 * i
-        begin_copy(t + 3)
-        begin_copy(t + 4)
-        finish_copy(t + 1)
-        finish_copy(t + 2)
-        load(t + 1, kwide_b, vwide_b)
-        attend(t, kd, vd)
-        spread(kwide_b, vwide_b, kd_b, vd_b)
-        load(t + 2, kwide, vwide)
-        attend(t + 1, kd_b, vd_b)
-        spread(kwide, vwide, kd, vd)
+        ready = [score(stage) for stage in stages[:LOOK]]
+        for index, (k, h) in enumerate(stages):
+            if index + LOOK < len(stages):
+                ready.append(score(stages[index + LOOK]))
+            s = jnp.where(pos < spots[k][1], ready[index], NEG)
+            m = jnp.maximum(jnp.max(s, axis=1, keepdims=True), FLOOR) * scale
+            p = jnp.exp2(s * scale - m).astype(jnp.bfloat16)
+            v = vd[k, h]
+            pv = jnp.dot(
+                p, jnp.concatenate([v, jnp.ones_like(v)], axis=1),
+                preferred_element_type=jnp.float32,
+            )
+            fold((k, h), m, pv)
         return carry
 
-    lax.fori_loop(0, (total + 1) // 2, body, 0)
+    lax.fori_loop(0, (total + BATCH - 1) // BATCH, body, 0)
 
 
 def with_suffix(accepted, cache_slot, history, qall, acc, den, top, sk, sv):
@@ -373,7 +379,7 @@
     slen = flat // heads
     chunk = min(slen, 256)
     wide = chunk * heads
-    depth = 4
+    depth = slots + BATCH
     vmem = pl.BlockSpec(memory_space=pltpu.VMEM)
     hbm = pl.BlockSpec(memory_space=pltpu.HBM)
     smem = pl.BlockSpec(memory_space=pltpu.SMEM)
@@ -387,8 +393,8 @@
             pltpu.VMEM((depth, wide, hd), jnp.bfloat16),
             pltpu.VMEM((depth, wide, hd), jnp.bfloat16),
         ]
-        + [pltpu.VMEM((wide, hd), jnp.float32)] * 4
-        + [pltpu.VMEM((heads, chunk, hd), jnp.bfloat16)] * 4
+        + [pltpu.VMEM((BATCH, wide, hd), jnp.float32)] * 2
+        + [pltpu.VMEM((BATCH, heads, chunk, hd), jnp.bfloat16)] * 2
         + [
             pltpu.SMEM((slots, 3), jnp.int32),
             pltpu.SMEM((slots * (slen // chunk), 2), jnp.int32),

time: 59.8 us -> 56.4 us (0.943); the launches traced: 60.5 us -> 56.3 us
  Pallas kernels: 58.8 us -> 54.5 us
    pallas_call x1, Pallas kernels: 16.8 us -> 10.9 us  [with_suffix(): pl.pallas_call(functools.partial(suffix_kernel, scale=LOG2E / math.sqrt(h...]
    pallas_call x1, Pallas kernels: 18 us -> 19.6 us  [reduced(): pl.pallas_call(functools.partial(reduce_kernel, n=n), out_shape=jax.Shape...]
where the time goes in v2:
time: 56.4 us; the launch traced here: 56.3 us
  Pallas kernels  54.5 us (97%)
  local copies, waits for them, and re-layouts  1.67 us (3%)
    pallas_call x1, Pallas kernels, gathered(): pl.pallas_call(functools.partial(gather_kernel, n=n, scale=LOG2E / math.s...  24 us
    pallas_call x1, Pallas kernels, reduced(): pl.pallas_call(functools.partial(reduce_kernel, n=n), out_shape=jax.Shape...  19.6 us
    pallas_call x1, Pallas kernels, with_suffix(): pl.pallas_call(functools.partial(suffix_kernel, scale=LOG2E / math.sqrt(h...  10.9 us
    unnamed x9, local copies, waits for them, and re-layouts  1.67 us

profile of v2, /device:TPU:0, one launch (start us, length us, event | category | flops | bytes accessed | tf_op | source)
XLA Modules:
  0.0 56.3 jit_solution(11189458839479411287)
XLA Ops:
  0.0 0.0 copy-start
  0.0 0.9 %copy-done = bf16[32,4,8,128]{3,2,1,0:T(8,128)(2,1)S(1)} copy-done((bf16[32,4,8,128]{3,2,1,0:T(8,128)(2,1)S(1)}, bf16[32,4,8,128]{3,2,1,0:T(8,128)(2,1)}, u32[]{:S(2)}) %copy-start) | copy-done | bytes 262168
  1.0 0.0 copy-start.1
  1.0 0.0 copy-start.2
  1.0 0.0 copy-start.3
  1.0 24.0 %shard_map.82 = (bf16[4,128,8,128]{3,2,1,0:T(8,128)(2,1)S(1)}, f32[4,128,8,128]{3,2,1,0:T(8,128)S(1)}, f32[4,128,8,128]{3,2,1,0:T(8,128)S(1)}, f32[4,128,8,128]{3,2,1,0:T(8,128)S(1)}) custom-call(bf16[32,4,8,128]{3,2,1,0:T(8,128)(2,1)S(1)} %copy-done, bf16[8192,128]{1,0:T(8,128)(2,1)} %bitcast.6, bf16[8192,128]{1,0:T(8,128)(2,1)} %bitcast.7), custom_call_target="tpu_custom_call" | custom-call | tf_op jit(solution)/shard_map/pallas_call | solution.py:216
  24.9 0.0 copy-done.1
  24.9 0.0 copy-done.2
  25.0 0.0 copy-done.3
  25.0 10.9 %shard_map.83 = (f32[4,128,8,128]{3,2,1,0:T(8,128)S(1)}, f32[4,128,8,128]{3,2,1,0:T(8,128)S(1)}, f32[4,128,8,128]{3,2,1,0:T(8,128)S(1)}) custom-call(s32[32]{0:T(128)S(1)} %copy-done.1, s32[32]{0:T(128)S(1)} %copy-done.2, s32[32]{0:T(128)S(1)} %copy-done.3, ...), custom_call_target="tpu_custom_call", output_to_operand_aliasing={{0}: (4, {}), {1}: (5, {}), {2}: (6, {})} | custom-call | tf_op jit(solution)/shard_map/pallas_call | solution.py:386
  35.9 19.6 %shard_map.84 = bf16[32,4,8,128]{3,2,1,0:T(8,128)(2,1)S(1)} custom-call(f32[4,128,8,128]{3,2,1,0:T(8,128)S(1)} %get-tuple-element.16.acc, f32[4,128,8,128]{3,2,1,0:T(8,128)S(1)} %get-tuple-element.17.den, f32[4,128,8,128]{3,2,1,0:T(8,128)S(1)} %get-tuple-element.18.top), custom_call_target="tpu_custom_call" | custom-call | tf_op jit(solution)/shard_map/pallas_call | solution.py:536
  55.5 0.7 %copy.16 = bf16[32,4,8,128]{3,2,1,0:T(8,128)(2,1)} copy(bf16[32,4,8,128]{3,2,1,0:T(8,128)(2,1)S(1)} %shard_map.84) | data formatting | bytes 524288
Async XLA Ops:
  0.0 0.9 %copy-start = (bf16[32,4,8,128]{3,2,1,0:T(8,128)(2,1)S(1)}, bf16[32,4,8,128]{3,2,1,0:T(8,128)(2,1)}, u32[]{:S(2)}) copy-start(bf16[32,4,8,128]{3,2,1,0:T(8,128)(2,1)} %q_hbm.1) | copy-start | bytes 786436
  1.0 24.0 %copy-start.1 = (s32[32]{0:T(128)S(1)}, s32[32]{0:T(128)}, u32[]{:S(2)}) copy-start(s32[32]{0:T(128)} %accepted.1) | copy-start | bytes 388
  1.0 24.0 %copy-start.2 = (s32[32]{0:T(128)S(1)}, s32[32]{0:T(128)}, u32[]{:S(2)}) copy-start(s32[32]{0:T(128)} %cache_slot.1) | copy-start | bytes 388
  1.0 24.0 %copy-start.3 = (s32[32]{0:T(128)S(1)}, s32[32]{0:T(128)}, u32[]{:S(2)}) copy-start(s32[32]{0:T(128)} %history.1) | copy-start | bytes 388

commit v3 on v2

--- a/solution.py
+++ b/solution.py
@@ -167,17 +167,21 @@
             def _():
                 own_copy(h).wait()
 
-            for side, there in outward:
-                source = p - k if side == 0 else p + k
-                landed = qall.at[h, block_at(source)]
-
-                @pl.when((k > 0) & (source >= 0) & (source < n))
-                def _(side=side, source=source, landed=landed, there=there):
-                    send(landed, side, source, h).wait_recv()
-
-                    @pl.when(there)
-                    def _():
-                        send(landed, side, source, h).start()
+            for wave in (k, k + 1):
+                lag = jnp.minimum(wave + 1, heads)
+                c = (k - wave + 1) * heads + h - lag
+                for side, there in outward:
+                    source = p - wave if side == 0 else p + wave
+                    due = (wave > 0) & (c >= 0) & (c < heads) & (source >= 0) & (source < n)
+
+                    @pl.when(due)
+                    def _(side=side, source=source, c=c, there=there):
+                        landed = qall.at[c, block_at(source)]
+                        send(landed, side, source, c).wait_recv()
+
+                        @pl.when(there)
+                        def _():
+                            send(landed, side, source, c).start()
 
         def load_q(h):
             return qall[h, block_at(b)].reshape(rows * gs, hd)

time: 56.4 us -> 57.1 us (1.012); the launches traced: 56.3 us -> 57.7 us
  Pallas kernels: 54.5 us -> 56 us
    pallas_call x1, Pallas kernels: 19.6 us -> 22.4 us  [reduced(): pl.pallas_call(functools.partial(reduce_kernel, n=n), out_shape=jax.Shape...]
    pallas_call x1, Pallas kernels: 10.9 us -> 9.44 us  [with_suffix(): pl.pallas_call(functools.partial(suffix_kernel, scale=LOG2E / math.sqrt(h...]
where the time goes in v3:
time: 57.1 us; the launch traced here: 57.7 us
  Pallas kernels  56 us (98%)
  local copies, waits for them, and re-layouts  1.67 us (3%)
    pallas_call x1, Pallas kernels, gathered(): pl.pallas_call(functools.partial(gather_kernel, n=n, scale=LOG2E / math.s...  24.1 us
    pallas_call x1, Pallas kernels, reduced(): pl.pallas_call(functools.partial(reduce_kernel, n=n), out_shape=jax.Shape...  22.4 us
    pallas_call x1, Pallas kernels, with_suffix(): pl.pallas_call(functools.partial(suffix_kernel, scale=LOG2E / math.sqrt(h...  9.44 us
    unnamed x9, local copies, waits for them, and re-layouts  1.67 us

profile of v3, /device:TPU:0, one launch (start us, length us, event | category | flops | bytes accessed | tf_op | source)
XLA Modules:
  0.0 57.7 jit_solution(18127124874538436691)
XLA Ops:
  0.0 0.0 copy-start
  0.0 0.9 %copy-done = bf16[32,4,8,128]{3,2,1,0:T(8,128)(2,1)S(1)} copy-done((bf16[32,4,8,128]{3,2,1,0:T(8,128)(2,1)S(1)}, bf16[32,4,8,128]{3,2,1,0:T(8,128)(2,1)}, u32[]{:S(2)}) %copy-start) | copy-done | bytes 262168
  1.0 0.0 copy-start.1
  1.0 0.0 copy-start.2
  1.0 0.0 copy-start.3
  1.0 24.1 %shard_map.82 = (bf16[4,128,8,128]{3,2,1,0:T(8,128)(2,1)S(1)}, f32[4,128,8,128]{3,2,1,0:T(8,128)S(1)}, f32[4,128,8,128]{3,2,1,0:T(8,128)S(1)}, f32[4,128,8,128]{3,2,1,0:T(8,128)S(1)}) custom-call(bf16[32,4,8,128]{3,2,1,0:T(8,128)(2,1)S(1)} %copy-done, bf16[8192,128]{1,0:T(8,128)(2,1)} %bitcast.6, bf16[8192,128]{1,0:T(8,128)(2,1)} %bitcast.7), custom_call_target="tpu_custom_call" | custom-call | tf_op jit(solution)/shard_map/pallas_call | solution.py:220
  25.1 0.0 copy-done.1
  25.1 0.0 copy-done.2
  25.1 0.0 copy-done.3
  25.1 9.4 %shard_map.83 = (f32[4,128,8,128]{3,2,1,0:T(8,128)S(1)}, f32[4,128,8,128]{3,2,1,0:T(8,128)S(1)}, f32[4,128,8,128]{3,2,1,0:T(8,128)S(1)}) custom-call(s32[32]{0:T(128)S(1)} %copy-done.1, s32[32]{0:T(128)S(1)} %copy-done.2, s32[32]{0:T(128)S(1)} %copy-done.3, ...), custom_call_target="tpu_custom_call", output_to_operand_aliasing={{0}: (4, {}), {1}: (5, {}), {2}: (6, {})} | custom-call | tf_op jit(solution)/shard_map/pallas_call | solution.py:390
  34.6 22.4 %shard_map.84 = bf16[32,4,8,128]{3,2,1,0:T(8,128)(2,1)S(1)} custom-call(f32[4,128,8,128]{3,2,1,0:T(8,128)S(1)} %get-tuple-element.16.acc, f32[4,128,8,128]{3,2,1,0:T(8,128)S(1)} %get-tuple-element.17.den, f32[4,128,8,128]{3,2,1,0:T(8,128)S(1)} %get-tuple-element.18.top), custom_call_target="tpu_custom_call" | custom-call | tf_op jit(solution)/shard_map/pallas_call | solution.py:540
  57.0 0.7 %copy.16 = bf16[32,4,8,128]{3,2,1,0:T(8,128)(2,1)} copy(bf16[32,4,8,128]{3,2,1,0:T(8,128)(2,1)S(1)} %shard_map.84) | data formatting | bytes 524288
Async XLA Ops:
  0.0 0.9 %copy-start = (bf16[32,4,8,128]{3,2,1,0:T(8,128)(2,1)S(1)}, bf16[32,4,8,128]{3,2,1,0:T(8,128)(2,1)}, u32[]{:S(2)}) copy-start(bf16[32,4,8,128]{3,2,1,0:T(8,128)(2,1)} %q_hbm.1) | copy-start | bytes 786436
  1.0 24.1 %copy-start.1 = (s32[32]{0:T(128)S(1)}, s32[32]{0:T(128)}, u32[]{:S(2)}) copy-start(s32[32]{0:T(128)} %accepted.1) | copy-start | bytes 388
  1.0 24.2 %copy-start.2 = (s32[32]{0:T(128)S(1)}, s32[32]{0:T(128)}, u32[]{:S(2)}) copy-start(s32[32]{0:T(128)} %cache_slot.1) | copy-start | bytes 388
  1.0 24.2 %copy-start.3 = (s32[32]{0:T(128)S(1)}, s32[32]{0:T(128)}, u32[]{:S(2)}) copy-start(s32[32]{0:T(128)} %history.1) | copy-start | bytes 388

commit v4 on v3

--- a/solution.py
+++ b/solution.py
@@ -14,7 +14,7 @@
 LOG2E = 1.4426950408889634
 VMEM = 67043328
 STAGGER = 2
-BATCH = 4
+BATCH = 2
 LOOK = 2
 SPARE = 12 * 1024 * 1024
 MESH = pl.DeviceIdType.MESH
@@ -383,7 +383,7 @@
     slen = flat // heads
     chunk = min(slen, 256)
     wide = chunk * heads
-    depth = slots + BATCH
+    depth = slots + 2 * BATCH
     vmem = pl.BlockSpec(memory_space=pltpu.VMEM)
     hbm = pl.BlockSpec(memory_space=pltpu.HBM)
     smem = pl.BlockSpec(memory_space=pltpu.SMEM)

time: 57.1 us -> 56.3 us (0.986); the launches traced: 57.7 us -> 55.7 us
  Pallas kernels: 56 us -> 54 us
    pallas_call x1, Pallas kernels: 22.4 us -> 19.6 us  [reduced(): pl.pallas_call(functools.partial(reduce_kernel, n=n), out_shape=jax.Shape...]
    pallas_call x1, Pallas kernels: 9.44 us -> 10.3 us  [with_suffix(): pl.pallas_call(functools.partial(suffix_kernel, scale=LOG2E / math.sqrt(h...]
where the time goes in v4:
time: 56.3 us; the launch traced here: 55.7 us
  Pallas kernels  54 us (96%)
  local copies, waits for them, and re-layouts  1.67 us (3%)
    pallas_call x1, Pallas kernels, gathered(): pl.pallas_call(functools.partial(gather_kernel, n=n, scale=LOG2E / math.s...  24.1 us
    pallas_call x1, Pallas kernels, reduced(): pl.pallas_call(functools.partial(reduce_kernel, n=n), out_shape=jax.Shape...  19.6 us
    pallas_call x1, Pallas kernels, with_suffix(): pl.pallas_call(functools.partial(suffix_kernel, scale=LOG2E / math.sqrt(h...  10.3 us
    unnamed x9, local copies, waits for them, and re-layouts  1.67 us

profile of v4, /device:TPU:0, one launch (start us, length us, event | category | flops | bytes accessed | tf_op | source)
XLA Modules:
  0.0 55.7 jit_solution(11796817345252757239)
XLA Ops:
  0.0 0.0 copy-start
  0.0 0.9 %copy-done = bf16[32,4,8,128]{3,2,1,0:T(8,128)(2,1)S(1)} copy-done((bf16[32,4,8,128]{3,2,1,0:T(8,128)(2,1)S(1)}, bf16[32,4,8,128]{3,2,1,0:T(8,128)(2,1)}, u32[]{:S(2)}) %copy-start) | copy-done | bytes 262168
  1.0 0.0 copy-start.1
  1.0 0.0 copy-start.2
  1.0 0.0 copy-start.3
  1.0 24.1 %shard_map.82 = (bf16[4,128,8,128]{3,2,1,0:T(8,128)(2,1)S(1)}, f32[4,128,8,128]{3,2,1,0:T(8,128)S(1)}, f32[4,128,8,128]{3,2,1,0:T(8,128)S(1)}, f32[4,128,8,128]{3,2,1,0:T(8,128)S(1)}) custom-call(bf16[32,4,8,128]{3,2,1,0:T(8,128)(2,1)S(1)} %copy-done, bf16[8192,128]{1,0:T(8,128)(2,1)} %bitcast.6, bf16[8192,128]{1,0:T(8,128)(2,1)} %bitcast.7), custom_call_target="tpu_custom_call" | custom-call | tf_op jit(solution)/shard_map/pallas_call | solution.py:220
  25.1 0.0 copy-done.1
  25.1 0.0 copy-done.2
  25.1 0.0 copy-done.3
  25.1 10.3 %shard_map.83 = (f32[4,128,8,128]{3,2,1,0:T(8,128)S(1)}, f32[4,128,8,128]{3,2,1,0:T(8,128)S(1)}, f32[4,128,8,128]{3,2,1,0:T(8,128)S(1)}) custom-call(s32[32]{0:T(128)S(1)} %copy-done.1, s32[32]{0:T(128)S(1)} %copy-done.2, s32[32]{0:T(128)S(1)} %copy-done.3, ...), custom_call_target="tpu_custom_call", output_to_operand_aliasing={{0}: (4, {}), {1}: (5, {}), {2}: (6, {})} | custom-call | tf_op jit(solution)/shard_map/pallas_call | solution.py:390
  35.4 19.6 %shard_map.84 = bf16[32,4,8,128]{3,2,1,0:T(8,128)(2,1)S(1)} custom-call(f32[4,128,8,128]{3,2,1,0:T(8,128)S(1)} %get-tuple-element.16.acc, f32[4,128,8,128]{3,2,1,0:T(8,128)S(1)} %get-tuple-element.17.den, f32[4,128,8,128]{3,2,1,0:T(8,128)S(1)} %get-tuple-element.18.top), custom_call_target="tpu_custom_call" | custom-call | tf_op jit(solution)/shard_map/pallas_call | solution.py:540
  55.0 0.7 %copy.16 = bf16[32,4,8,128]{3,2,1,0:T(8,128)(2,1)} copy(bf16[32,4,8,128]{3,2,1,0:T(8,128)(2,1)S(1)} %shard_map.84) | data formatting | bytes 524288
Async XLA Ops:
  0.0 0.9 %copy-start = (bf16[32,4,8,128]{3,2,1,0:T(8,128)(2,1)S(1)}, bf16[32,4,8,128]{3,2,1,0:T(8,128)(2,1)}, u32[]{:S(2)}) copy-start(bf16[32,4,8,128]{3,2,1,0:T(8,128)(2,1)} %q_hbm.1) | copy-start | bytes 786436
  1.0 24.1 %copy-start.1 = (s32[32]{0:T(128)S(1)}, s32[32]{0:T(128)}, u32[]{:S(2)}) copy-start(s32[32]{0:T(128)} %accepted.1) | copy-start | bytes 388
  1.0 24.2 %copy-start.2 = (s32[32]{0:T(128)S(1)}, s32[32]{0:T(128)}, u32[]{:S(2)}) copy-start(s32[32]{0:T(128)} %cache_slot.1) | copy-start | bytes 388
  1.0 24.2 %copy-start.3 = (s32[32]{0:T(128)S(1)}, s32[32]{0:T(128)}, u32[]{:S(2)}) copy-start(s32[32]{0:T(128)} %history.1) | copy-start | bytes 388
